TPU v7x, 256 devices: a whole 4x4x8 slice. The times are simulated.
256 devices in a mesh: seq: 32 (over y, z_lo, core), head: 8 (over x, z_hi).
Axes of the slice: x: 4, y: 4, z: 8 (z_hi: 2, z_lo: 4; z = z_hi * 4 + z_lo), core: 2. Of those that a mesh axis runs over, the one named last changes fastest.
Arguments:
- queries: bfloat16 [4096, 8192], P('seq', 'head'), may hold values from -48 to 48
- keyval: bfloat16 [4096, 2048], P('seq', 'head'), may hold values from -48 to 48
- grad_out: bfloat16 [4096, 8192], P('seq', 'head'), may hold values from -6 to 6
- doc_ids: int32 [4096], P('seq'), may hold values from 0 to 3, never falling along the last dimension, each value on 1 to 2048 neighbouring positions
- deltas: bfloat16 [8, 4096, 8192], P('head', 'seq'), may hold values from -6 to 6
- node_weights: bfloat16 [8192, 2048], P('head', 'seq'), may hold values from -0.0625 to 0.0625
- layer_slot: int32 [8], replicated, may hold values from 0 to 7, each once
Outputs:
- grad_query: bfloat16 [4096, 8192], P('seq', 'head')
- grad_keyval: bfloat16 [4096, 2048], P('seq', 'head')
- scores: float32 [8, 16], replicated
Inputs may be any that keep to these rules, and one draw needn't show every extreme that they name: `layer_slot`: each of the 8 layers stands in exactly one slot. `doc_ids`: never falling along the sequence.
All inputs are finite; a program needn't handle non-finite values.
Results may differ from a plain program's by a relative error of at most 0.013.
Values may be sent and summed in bfloat16 or wider, within the bound.
A program may use at most 64 MiB of HBM per device.

v0:
```python
import math
import jax
import jax.numpy as jnp
from jax import lax
from jax.sharding import PartitionSpec as P

H = 64
KVH = 8
HD = 128


def over_blocks(step, carry, pieces):
    total_rows = pieces[0].shape[0]
    block_rows = 512

    def one_turn(turn_index, running):
        offset = turn_index * block_rows
        blocks = tuple((lax.dynamic_slice_in_dim(piece, offset, block_rows, 0) for piece in pieces))
        return step(running, *blocks, offset)

    return lax.fori_loop(0, total_rows // block_rows, one_turn, carry)


def on_device(queries, keyval, grad_out, doc_ids, deltas, node_weights, layer_slot):
    tok_rows = queries.shape[0]
    kv_local = keyval.shape[1] // (2 * HD)
    group_size = H // KVH
    score_scale = 1.0 / math.sqrt(HD)
    seq_total = tok_rows * lax.axis_size("seq")
    query_grid = queries.reshape(tok_rows, kv_local, group_size, HD)
    out_grid = grad_out.reshape(tok_rows, kv_local, group_size, HD)
    row_positions = lax.axis_index("seq") * tok_rows + jnp.arange(tok_rows, dtype=jnp.int32)

    def block_logits(kv_rows, key_ids, key_start):
        width = kv_rows.shape[0]
        kv_grid = kv_rows.reshape(width, kv_local, 2, HD)
        logits = (
            jnp.einsum(
                "tgie,rge->gitr", query_grid, kv_grid[:, :, 0], preferred_element_type=jnp.float32
            )
            * score_scale
        )
        key_positions = key_start + jnp.arange(width, dtype=jnp.int32)
        allowed = (key_ids[None, :] == doc_ids[:, None]) & (
            key_positions[None, :] <= row_positions[:, None]
        )
        return (logits, allowed, kv_grid)

    def forward_step(carry, kv_rows, key_ids, key_start):
        run_max, run_sum, accum = carry
        logits, allowed, kv_grid = block_logits(kv_rows, key_ids, key_start)
        new_max = jnp.maximum(run_max, jnp.max(jnp.where(allowed, logits, -1e30), axis=3))
        weights = jnp.where(allowed, jnp.exp(logits - new_max[..., None]), 0.0)
        factor = jnp.exp(run_max - new_max)
        run_sum = run_sum * factor + jnp.sum(weights, axis=3)
        values = kv_grid[:, :, 1].astype(jnp.float32)
        accum = accum * factor[..., None] + jnp.einsum(
            "gitr,rge->gite", weights, values, precision=lax.Precision.HIGHEST
        )
        return (new_max, run_sum, accum)

    stat_shape = (kv_local, group_size, tok_rows)
    forward_init = (
        jnp.full(stat_shape, -1e30, jnp.float32),
        jnp.zeros(stat_shape, jnp.float32),
        jnp.zeros(stat_shape + (HD,), jnp.float32),
    )
    run_max, run_sum, accum = over_blocks(
        forward_step,
        forward_init,
        (
            lax.all_gather(keyval, "seq", axis=0, tiled=True),
            lax.all_gather(doc_ids, "seq", axis=0, tiled=True),
        ),
    )
    log_total = run_max + jnp.log(run_sum)
    attn_out = accum / run_sum[..., None]
    row_dot = jnp.einsum(
        "tgie,gite->git", out_grid.astype(jnp.float32), attn_out, precision=lax.Precision.HIGHEST
    )

    def backward_step(carry, kv_rows, key_ids, key_start):
        query_accum = carry[0]
        width = kv_rows.shape[0]
        logits, allowed, kv_grid = block_logits(kv_rows, key_ids, key_start)
        probs = jnp.where(allowed, jnp.exp(logits - log_total[..., None]), 0.0)
        grad_probs = jnp.einsum(
            "tgie,rge->gitr", out_grid, kv_grid[:, :, 1], preferred_element_type=jnp.float32
        )
        grad_logits = (probs * (grad_probs - row_dot[..., None])).astype(jnp.bfloat16)
        query_accum = (
            query_accum
            + jnp.einsum(
                "gitr,rge->gite", grad_logits, kv_grid[:, :, 0], preferred_element_type=jnp.float32
            )
            * score_scale
        )
        probs_low = probs.astype(jnp.bfloat16)
        grad_keys = (
            jnp.einsum(
                "gitr,tgie->rge", grad_logits, query_grid, preferred_element_type=jnp.float32
            )
            * score_scale
        )
        grad_values = jnp.einsum(
            "gitr,tgie->rge", probs_low, out_grid, preferred_element_type=jnp.float32
        )
        block_grad = jnp.stack((grad_keys, grad_values), axis=2).reshape(width, kv_local * 2 * HD)
        kv_buffer = lax.dynamic_update_slice(
            carry[1], block_grad, (key_start, jnp.zeros((), jnp.int32))
        )
        return (query_accum, kv_buffer)

    query_zero = jnp.zeros(stat_shape + (HD,), jnp.float32)
    backward_init = (query_zero, jnp.zeros((seq_total, kv_local * 2 * HD), jnp.float32))
    backward_out = over_blocks(
        backward_step,
        backward_init,
        (
            lax.all_gather(keyval, "seq", axis=0, tiled=True),
            lax.all_gather(doc_ids, "seq", axis=0, tiled=True),
        ),
    )
    query_accum = backward_out[0]
    grad_query = (
        jnp.transpose(query_accum, (2, 0, 1, 3))
        .reshape(tok_rows, kv_local * group_size * HD)
        .astype(jnp.bfloat16)
    )
    grad_keyval = lax.psum_scatter(
        backward_out[1].astype(jnp.bfloat16), "seq", scatter_dimension=0, tiled=True
    )
    width_deltas = lax.all_to_all(deltas, "head", split_axis=2, concat_axis=0, tiled=True)
    grad_rows = lax.all_gather(grad_keyval, "head", axis=1, tiled=True)
    layer_count = width_deltas.shape[0]
    node_count = grad_rows.shape[1] // HD
    projected = jnp.einsum(
        "ltd,dc->ltc",
        width_deltas,
        lax.all_gather(node_weights, "seq", axis=1, tiled=True),
        preferred_element_type=jnp.float32,
    )
    grad_cols = grad_rows.astype(jnp.float32)
    per_column = jnp.sum(projected * grad_cols[None], axis=1)
    partial_value = jnp.sum(per_column.reshape(layer_count, node_count, HD), axis=2)
    totals = lax.psum(partial_value / math.sqrt(seq_total), ("seq", "head"))
    placing = (layer_slot[:, None] == jnp.arange(layer_count, dtype=jnp.int32)[None, :]).astype(
        jnp.float32
    )
    scores = jnp.dot(placing.T, totals, precision=lax.Precision.HIGHEST)
    return (grad_query, grad_keyval, scores)


def solution(mesh):
    return jax.shard_map(
        on_device,
        mesh=mesh,
        in_specs=(
            P("seq", "head"),
            P("seq", "head"),
            P("seq", "head"),
            P("seq"),
            P("head", "seq", None),
            P("head", "seq"),
            P(),
        ),
        out_specs=(P("seq", "head"), P("seq", "head"), P()),
        check_vma=False,
    )
```

profile of v0, /device:TPU:1, one launch (start us, length us, event | category | flops | bytes accessed | tf_op | source)
XLA Modules:
  0.0 491.0 jit_solution(3479772316284741002)
XLA Ops:
  7.2 1.6 copy.67
  12.0 1.7 copy.96
  13.7 46.0 %all-gather = s32[32,1,128]{2,1,0:T(1,128)S(1)} all-gather(s32[1,1,128]{2,1,0:T(1,128)S(1)} %bitcast.262), channel_id=1, replica_groups=mesh['seq'=32,'head'=8] {'seq'}, dimensions={0}, use_global_device_ids=true | all-gather | bytes 16896 | tf_op jit(solution)/shard_map/all_gather | solution.py:121
  59.7 18.1 %all-gather.4.cloned.1.call-done = bf16[4096,256]{0,1:T(8,128)(2,1)} async-done(((bf16[128,256]{0,1:T(8,128)(2,1)}), bf16[4096,256]{0,1:T(8,128)(2,1)}) %all-gather.4.cloned.1.call-update) | async-done | bytes 2097168 | tf_op jit(solution)/shard_map/all_gather | solution.py:120
  77.8 55.1 %while.34 = (s32[]{:T(128)}, f32[1,8,128]{2,1,0:T(8,128)S(1)}, f32[1,8,128]{2,1,0:T(8,128)S(1)}, f32[1,8,128,128]{3,2,1,0:T(8,128)}, s32[4096]{0:T(1024)S(1)}, /...) while((s32[]{:T(128)}, f32[1,8,128]{2,1,0:T(8,128)S(1)}, ...), condition=%wide.region_3.4_spmd.clone, body=%wide.region_0.3_spmd.clone.sunk | while | flops 945363584 | bytes 8728263 | solution.py:21
  79.1 1.4 fusion.67
  80.6 2.8 fusion.70
  86.6 3.8 fusion.70
  92.1 1.4 fusion.67
  93.6 3.8 fusion.70
  100.6 3.8 fusion.70
  107.6 3.8 fusion.70
  113.2 1.4 fusion.67
  114.6 3.8 fusion.70
  120.2 1.4 fusion.67
  121.7 3.8 fusion.70
  127.2 1.4 fusion.67
  128.7 3.8 fusion.70
  135.6 1.6 broadcast_in_dim.87.clone
  137.2 39.6 %while.35 = (s32[]{:T(128)}, f32[1,8,128,128]{3,2,1,0:T(8,128)S(1)}, bf16[4096,256]{1,0:T(8,128)(2,1)}, s32[4096]{0:T(1024)S(1)}, s32[128]{0:T(128)S(1)}, /*inde...) while((s32[]{:T(128)}, ...), condition=%wide.region_5.6_spmd.clone, body=%wide.region_4.5_spmd.clone.sunk | while | flops 675611264 | bytes 14438105 | solution.py:21
  178.3 6.9 %copy.73 = bf16[1,128,8192]{1,0,2:T(2,128)(2,1)} copy(bf16[1,128,8192]{2,1,0:T(8,128)(2,1)S(1)} %copy-done) | data formatting | bytes 4194304 | tf_op args[4]
  185.7 45.2 %reduce.8 = bf16[8192,128]{1,0:T(8,128)(2,1)S(1)} reduce(bf16[8192,1,128]{2,1,0:T(2,128)(2,1)} %bitcast.245, bf16[]{:T(256)} %broadcast.122), dimensions={1}, to_apply=%bitcast.163.reduce_sub_computation | reduce | bytes 4194306
  230.9 3.2 reshape.216
  234.1 54.8 %all_to_all.18 = bf16[8,2,65536]{2,1,0:T(2,128)(2,1)S(1)} all-to-all(bf16[8,2,65536]{2,1,0:T(2,128)(2,1)} %reshape.216), channel_id=1, replica_groups=mesh['seq'=32,'head'=8] {'head'}, dimensions={0} | all-to-all | bytes 4194304 | tf_op jit(solution)/shard_map/all_to_all | solution.py:133
  288.9 4.4 reshape.217
  293.3 2.5 copy.93
  295.8 2.6 copy.74
  299.4 31.5 %reduce-scatter.2.cloned.1.call-done = bf16[128,256]{1,0:T(8,128)(2,1)} async-done(((bf16[4096,256]{1,0:T(8,128)(2,1)}), bf16[128,256]{1,0:T(8,128)(2,1)}) %reduce-scatter.2.cloned.1.call-update) | async-done | bytes 65552 | tf_op jit(solution)/shard_map/reduce_scatter | solution.py:130
  330.9 42.4 %all_gather.17 = bf16[128,2048]{1,0:T(8,128)(2,1)S(1)} all-gather(bf16[128,256]{1,0:T(8,128)(2,1)} %reduce-scatter.2.cloned.1.call-done), channel_id=1, replica_groups=mesh['seq'=32,'head'=8] {'head'}, dimensions={1}, use_global_device_ids=true | all-gather | bytes 589824 | tf_op jit(solution)/shard_map/all_gather | solution.py:134
  374.4 26.8 %all-gather.6.cloned.1.call-done = bf16[1024,2048]{0,1:T(8,128)(2,1)} async-done(((bf16[1024,64]{0,1:T(8,128)(2,1)}), bf16[1024,2048]{0,1:T(8,128)(2,1)}) %all-gather.6.cloned.1.call-update) | async-done | bytes 4194320 | tf_op jit(solution)/shard_map/all_gather | solution.py:140
  401.1 7.2 %multiply_reduce_fusion = f32[8,2048]{1,0:T(8,128)S(1)} fusion(bf16[1024,2048]{0,1:T(8,128)(2,1)} %all-gather.6.cloned.1.call-done, f32[128,2048]{1,0:T(8,128)} %convert_element_type.38, bf16[1,128,8,1024]{3,1,2,0:T(8,128)(2,1)S(1)} %copy-done.1), kind=kOutput, calls=%fused_computation.60 | convolution fusion | flops 4299145216 | bytes 7405568 | tf_op jit(solution)/shard_map/ltd,dc->ltc/dot_general | solution.py:137
  408.4 75.2 %psum.7 = f32[8,16]{0,1:T(8,128)S(1)} all-reduce(f32[8,16]{0,1:T(8,128)S(1)} %broadcast_multiply_fusion), channel_id=1, replica_groups=mesh['seq'=32,'head'=8] {'seq','head'}, use_global_device_ids=true, to_apply=%region_9.10 | all-reduce | flops 128 | bytes 1024 | tf_op jit(solution)/shard_map/psum | solution.py:146
  (212 shorter events, 67.9 us)
Async XLA Ops:
  7.2 6.6 %copy-start.2 = (s32[128]{0:T(128)S(1)}, s32[128]{0:T(128)}, u32[]{:S(2)}) copy-start(s32[128]{0:T(128)} %param.14) | copy-start | bytes 1540
  7.2 70.7 %all-gather.4.cloned.1.call-start = ((), (), s32[]{:S(2)}) async-start(), calls=%async_computation.2 | async-start | bytes 2162688 | tf_op jit(solution)/shard_map/all_gather | solution.py:120
  8.8 322.0 %reduce-scatter.2.cloned.1.call-start = ((), (), s32[]{:S(2)}) async-start(), calls=%async_computation.3 | async-start | bytes 2162688 | tf_op jit(solution)/shard_map/reduce_scatter | solution.py:130
  176.8 1.6 copy-start
  176.8 224.4 %all-gather.6.cloned.1.call-start = ((), (), s32[]{:S(2)}) async-start(), calls=%async_computation.4 | async-start | bytes 4325376 | tf_op jit(solution)/shard_map/all_gather | solution.py:140
  298.4 102.7 %copy-start.1 = (bf16[1,128,8,1024]{3,1,2,0:T(8,128)(2,1)S(1)}, bf16[1,128,8,1024]{3,1,2,0:T(8,128)(2,1)}, u32[]{:S(2)}) copy-start(bf16[1,128,8,1024]{3,1,2,0:T(8,128)(2,1)} %copy.74) | copy-start | bytes 6291460
  374.4 109.2 %copy-start.3 = (s32[8]{0:T(128)S(1)}, s32[8]{0:T(128)}, u32[]{:S(2)}) copy-start(s32[8]{0:T(128)} %param.17) | copy-start | bytes 100
Sparse Core Ops, SparseCore 0:
  10.3 67.4 all-gather.3
  176.9 153.8 reduce-scatter.1
  332.7 68.3 all-gather.5
where the time goes:
time: 493 us; the launch traced here: 491 us
  blocking collectives  218 us (44%)
  waiting for transfers between devices  76.9 us (16%)
  matrix products  70.4 us (14%)
  other arithmetic  56.2 us (11%)
  local copies, waits for them, and re-layouts  53.6 us (11%)
  between operations  13.9 us (3%)
    psum x1, blocking collectives, on_device(): totals = lax.psum(partial_value / math.sqrt(seq_total), ('seq', 'head'))  75.2 us
    all_to_all x1, blocking collectives, on_device(): lax.all_to_all(deltas, 'head', split_axis=2, concat_axis=0, tiled=True)  54.8 us
    unnamed x6, other arithmetic  46.5 us
    all_gather x1, blocking collectives, on_device(): lax.all_gather(doc_ids, 'seq', axis=0, tiled=True)  46 us
    all_gather x1, blocking collectives, on_device(): grad_rows = lax.all_gather(grad_keyval, 'head', axis=1, tiled=True)  42.4 us
    reduce_scatter x1, waiting for transfers between devices, on_device(): lax.psum_scatter(backward_out[1].astype(jnp.bfloat16), 'seq', scatter_dim...  31.5 us
    dot_general x8, matrix products, forward_step(): jnp.einsum('gitr,rge->gite', weights, values, precision=lax.Precision.HIG...  29.4 us
    all_gather x1, waiting for transfers between devices, on_device(): lax.all_gather(node_weights, 'seq', axis=1, tiled=True)  26.8 us
  transfers between devices with their start and end apart: 3, of which 3 were waited for; matrix products, arithmetic and copies ran while one was open for 15% of the time, Pallas kernels for 0%

commit v1 on v0

--- a/solution.py
+++ b/solution.py
@@ -143,7 +143,7 @@
     grad_cols = grad_rows.astype(jnp.float32)
     per_column = jnp.sum(projected * grad_cols[None], axis=1)
     partial_value = jnp.sum(per_column.reshape(layer_count, node_count, HD), axis=2)
-    totals = lax.psum(partial_value / math.sqrt(seq_total), ("seq", "head"))
+    totals = jnp.sum(lax.all_gather(partial_value / math.sqrt(seq_total), ("seq", "head")), axis=0)
     placing = (layer_slot[:, None] == jnp.arange(layer_count, dtype=jnp.int32)[None, :]).astype(
         jnp.float32
     )

time: 493 us -> 1090 us (2.21)
  blocking collectives: 218 us -> 814 us
    all_gather x0 -> x1, blocking collectives: none -> 671 us  [on_device(): lax.all_gather(partial_value / math.sqrt(seq_total), ('seq', 'head'))]
    psum x1 -> x0, blocking collectives: 75.2 us -> none  [on_device(): totals = lax.psum(partial_value / math.sqrt(seq_total), ('seq', 'head'))]
  transfers between devices with their start and end apart: 3 -> 3, of which waited for: 3 -> 3; matrix products, arithmetic and copies ran while one was open for 15% -> 7% of each run, Pallas kernels for 0% -> 0%
where the time goes in v1:
time: 1090 us
  blocking collectives  814 us (75%)
  waiting for transfers between devices  75.7 us (7%)
  matrix products  70.4 us (6%)
  other arithmetic  56.5 us (5%)
  local copies, waits for them, and re-layouts  53.7 us (5%)
  between operations  13.9 us (1%)
    all_gather x1, blocking collectives, on_device(): lax.all_gather(partial_value / math.sqrt(seq_total), ('seq', 'head'))  671 us
    all_to_all x1, blocking collectives, on_device(): lax.all_to_all(deltas, 'head', split_axis=2, concat_axis=0, tiled=True)  54.3 us
    unnamed x6, other arithmetic  46.5 us
    all_gather x1, blocking collectives, on_device(): lax.all_gather(doc_ids, 'seq', axis=0, tiled=True)  46 us
    all_gather x1, blocking collectives, on_device(): grad_rows = lax.all_gather(grad_keyval, 'head', axis=1, tiled=True)  42.8 us
    reduce_scatter x1, waiting for transfers between devices, on_device(): lax.psum_scatter(backward_out[1].astype(jnp.bfloat16), 'seq', scatter_dim...  33 us
    dot_general x8, matrix products, forward_step(): jnp.einsum('gitr,rge->gite', weights, values, precision=lax.Precision.HIG...  29.4 us
    unnamed x19, local copies, waits for them, and re-layouts  25.4 us
  transfers between devices with their start and end apart: 3, of which 3 were waited for; matrix products, arithmetic and copies ran while one was open for 7% of the time, Pallas kernels for 0%

profile of v1, /device:TPU:1, one launch (start us, length us, event | category | flops | bytes accessed | tf_op | source)
XLA Modules:
  0.0 1085.8 jit_solution(297777216696757390)
XLA Ops:
  7.2 1.6 copy.126
  12.0 1.7 copy.159
  13.7 46.0 %all-gather.1 = s32[32,1,128]{2,1,0:T(1,128)S(1)} all-gather(s32[1,1,128]{2,1,0:T(1,128)S(1)} %bitcast.264), channel_id=1, replica_groups=mesh['seq'=32,'head'=8] {'seq'}, dimensions={0}, use_global_device_ids=true | all-gather | bytes 16896 | tf_op jit(solution)/shard_map/all_gather | solution.py:121
  59.7 18.1 %all-gather.5.cloned.1.call-done = bf16[4096,256]{0,1:T(8,128)(2,1)} async-done(((bf16[128,256]{0,1:T(8,128)(2,1)}), bf16[4096,256]{0,1:T(8,128)(2,1)}) %all-gather.5.cloned.1.call-update) | async-done | bytes 2097168 | tf_op jit(solution)/shard_map/all_gather | solution.py:120
  77.8 55.1 %while.34 = (s32[]{:T(128)}, f32[1,8,128]{2,1,0:T(8,128)S(1)}, f32[1,8,128]{2,1,0:T(8,128)S(1)}, f32[1,8,128,128]{3,2,1,0:T(8,128)}, s32[4096]{0:T(1024)S(1)}, /...) while((s32[]{:T(128)}, f32[1,8,128]{2,1,0:T(8,128)S(1)}, ...), condition=%wide.region_3.4_spmd.clone, body=%wide.region_0.3_spmd.clone.sunk | while | flops 945363584 | bytes 8728263 | solution.py:21
  80.6 2.8 fusion.68
  85.1 1.4 fusion.65
  86.6 3.8 fusion.68
  93.6 3.8 fusion.68
  100.6 3.8 fusion.68
  106.2 1.4 fusion.65
  107.6 3.8 fusion.68
  113.2 1.4 fusion.65
  114.6 3.8 fusion.68
  120.2 1.4 fusion.65
  121.7 3.8 fusion.68
  127.2 1.4 fusion.65
  128.7 3.8 fusion.68
  135.6 1.6 broadcast_in_dim.87.clone
  137.2 39.6 %while.35 = (s32[]{:T(128)}, f32[1,8,128,128]{3,2,1,0:T(8,128)S(1)}, bf16[4096,256]{1,0:T(8,128)(2,1)}, s32[4096]{0:T(1024)S(1)}, s32[128]{0:T(128)S(1)}, /*inde...) while((s32[]{:T(128)}, ...), condition=%wide.region_5.6_spmd.clone, body=%wide.region_4.5_spmd.clone.sunk | while | flops 675611264 | bytes 14438105 | solution.py:21
  178.3 6.9 copy.132
  185.7 45.2 %reduce.8 = bf16[8192,128]{1,0:T(8,128)(2,1)S(1)} reduce(bf16[8192,1,128]{2,1,0:T(2,128)(2,1)} %bitcast.247, bf16[]{:T(256)} %broadcast.131), dimensions={1}, to_apply=%bitcast.165.reduce_sub_computation | reduce | bytes 4194306
  230.9 3.2 reshape.226
  234.1 54.3 %all_to_all.18 = bf16[8,2,65536]{2,1,0:T(2,128)(2,1)S(1)} all-to-all(bf16[8,2,65536]{2,1,0:T(2,128)(2,1)} %reshape.226), channel_id=1, replica_groups=mesh['seq'=32,'head'=8] {'head'}, dimensions={0} | all-to-all | bytes 4194304 | tf_op jit(solution)/shard_map/all_to_all | solution.py:133
  288.4 4.4 reshape.227
  292.8 2.5 copy.154
  295.3 2.6 copy.133
  298.9 33.0 %reduce-scatter.2.cloned.1.call-done = bf16[128,256]{1,0:T(8,128)(2,1)} async-done(((bf16[4096,256]{1,0:T(8,128)(2,1)}), bf16[128,256]{1,0:T(8,128)(2,1)}) %reduce-scatter.2.cloned.1.call-update) | async-done | bytes 65552 | tf_op jit(solution)/shard_map/reduce_scatter | solution.py:130
  331.9 42.8 %all_gather.21 = bf16[128,2048]{1,0:T(8,128)(2,1)S(1)} all-gather(bf16[128,256]{1,0:T(8,128)(2,1)} %reduce-scatter.2.cloned.1.call-done), channel_id=1, replica_groups=mesh['seq'=32,'head'=8] {'head'}, dimensions={1}, use_global_device_ids=true | all-gather | bytes 589824 | tf_op jit(solution)/shard_map/all_gather | solution.py:134
  375.9 24.0 %all-gather.7.cloned.1.call-done = bf16[1024,2048]{0,1:T(8,128)(2,1)} async-done(((bf16[1024,64]{0,1:T(8,128)(2,1)}), bf16[1024,2048]{0,1:T(8,128)(2,1)}) %all-gather.7.cloned.1.call-update) | async-done | bytes 4194320 | tf_op jit(solution)/shard_map/all_gather | solution.py:140
  399.8 7.2 multiply_reduce_fusion
  407.2 670.9 %all-gather = f32[2048,16]{1,0:T(8,128)S(1)} all-gather(f32[8,16]{1,0:T(8,128)S(1)} %broadcast_multiply_fusion), channel_id=2, replica_groups=mesh['seq'=32,'head'=8] {'seq','head'}, dimensions={0}, use_global_device_ids=true | all-gather | bytes 131584 | tf_op jit(solution)/shard_map/all_gather | solution.py:146
  (214 shorter events, 68.2 us)
Async XLA Ops:
  7.2 6.6 copy-start.2
  7.2 70.7 %all-gather.5.cloned.1.call-start = ((), (), s32[]{:S(2)}) async-start(), calls=%async_computation.2 | async-start | bytes 2162688 | tf_op jit(solution)/shard_map/all_gather | solution.py:120
  8.8 323.1 %reduce-scatter.2.cloned.1.call-start = ((), (), s32[]{:S(2)}) async-start(), calls=%async_computation.3 | async-start | bytes 2162688 | tf_op jit(solution)/shard_map/reduce_scatter | solution.py:130
  176.8 1.6 copy-start
  176.8 223.1 %all-gather.7.cloned.1.call-start = ((), (), s32[]{:S(2)}) async-start(), calls=%async_computation.4 | async-start | bytes 4325376 | tf_op jit(solution)/shard_map/all_gather | solution.py:140
  297.9 101.9 %copy-start.1 = (bf16[1,128,8,1024]{3,1,2,0:T(8,128)(2,1)S(1)}, bf16[1,128,8,1024]{3,1,2,0:T(8,128)(2,1)}, u32[]{:S(2)}) copy-start(bf16[1,128,8,1024]{3,1,2,0:T(8,128)(2,1)} %copy.133) | copy-start | bytes 6291460
  407.0 671.4 %copy-start.3 = (s32[8]{0:T(128)S(1)}, s32[8]{0:T(128)}, u32[]{:S(2)}) copy-start(s32[8]{0:T(128)} %param.17) | copy-start | bytes 100
Sparse Core Ops, SparseCore 0:
  10.3 67.4 all-gather.4
  176.9 154.9 reduce-scatter.1
  333.8 65.9 all-gather.6
